TPU v7x, 32 devices: a whole 2x2x4 slice. The times are simulated.
32 devices in a mesh: row: 8 (over y, x, core), col: 4 (over z).
Axes of the slice: x: 2, y: 2, z: 4, core: 2. Of those that a mesh axis runs over, the one named last changes fastest.
Arguments:
- covariance: float32 [8192, 8192], P('row', 'col'), as said below
- innovations: float32 [512, 8, 1024], P('row', None, 'col'), may hold values from -6 to 6
- block_owner: int32 [32], replicated, may hold values from 0 to 31, as said below
- panel_index: int32 [1], replicated, may hold values from 0 to 15
Outputs:
- factor: float32 [8192, 8192], P('row', 'col')
- solved: float32 [512, 8192], P('col', 'row')
Inputs may be any that keep to these rules, and one draw needn't show every extreme that they name: Storage block s holds global block block_owner[s]; every global block appears once; the storage blocks s with one value of s // 4 hold the blocks of one residue modulo 8, rising with s. `covariance`: symmetric positive definite.
All inputs are finite; a program needn't handle non-finite values.
Results may differ from a plain program's by a relative error of at most 0.0016.
Values may be sent and summed in bfloat16 or wider, within the bound.
A program may use at most 128 MiB of HBM per device.

v0:
```python
import jax
import jax.numpy as jnp
from jax import lax
from jax.sharding import PartitionSpec as P

B = 256
PANELS = 2
CONTRACT_LAST = (((1,), (1,)), ((), ()))


def spread(value, axis, source):
    kept = jnp.where(lax.axis_index(axis) == source, value, 0).astype(value.dtype)
    return lax.psum(kept, axis)


def lower_solve(factor, right_side):
    return jax.scipy.linalg.solve_triangular(factor, right_side, lower=True)


def outer_rows(left, right):
    return lax.dot_general(left, right, CONTRACT_LAST, preferred_element_type=jnp.float32)


def locate(block_owner, target):
    positions = jnp.arange(block_owner.shape[0], dtype=jnp.int32)
    return jnp.sum(jnp.where(block_owner == target, positions, 0))


def per_device(covariance, innovations, block_owner, panel_index):
    panel_width = B
    local_rows, local_cols = covariance.shape
    row_blocks = local_rows // panel_width
    column_blocks = local_cols // panel_width
    row_here = lax.axis_index("row")
    column_here = lax.axis_index("col")
    relaid = lax.all_to_all(
        lax.all_to_all(innovations, "row", split_axis=1, concat_axis=0, tiled=True),
        "col",
        split_axis=0,
        concat_axis=2,
        tiled=True,
    )
    solved = relaid.reshape(relaid.shape[0], local_rows)
    owner_rows = jnp.repeat(
        lax.dynamic_slice_in_dim(block_owner, row_here * row_blocks, row_blocks), panel_width
    )
    owner_columns = jnp.repeat(
        lax.dynamic_slice_in_dim(block_owner, column_here * column_blocks, column_blocks),
        panel_width,
    )
    matrix = covariance
    ahead_column = None
    for panel_turn in range(PANELS):
        target = panel_index[0] + panel_turn
        slot_index = locate(block_owner, target)
        row_root = slot_index // row_blocks
        column_root = slot_index // column_blocks
        row_start = slot_index % row_blocks * panel_width
        column_start = slot_index % column_blocks * panel_width
        column_local = lax.dynamic_slice_in_dim(matrix, column_start, panel_width, 1)
        ahead_column = None
        live_rows = owner_rows > target
        live_columns = owner_columns > target
        column = spread(column_local, "col", column_root)
        diagonal_local = lax.dynamic_slice_in_dim(column, row_start, panel_width, 0)
        innovation_local = lax.dynamic_slice_in_dim(solved, row_start, panel_width, 1)
        diagonal, innovation_block = (
            spread(diagonal_local, "row", row_root),
            spread(innovation_local, "row", row_root),
        )
        factor = jnp.linalg.cholesky(diagonal)
        panel_rows = jnp.where(live_rows[:, None], lower_solve(factor, column.T).T, 0.0)
        rows_half = panel_rows.astype(jnp.bfloat16)
        row_local = lax.dynamic_slice_in_dim(matrix, row_start, panel_width, 0)
        row_panel = spread(row_local, "row", row_root)
        panel_columns = jnp.where(live_columns[:, None], lower_solve(factor, row_panel).T, 0.0)
        columns_half = panel_columns.astype(jnp.bfloat16)
        matrix = matrix - outer_rows(rows_half, columns_half)
        whitened = lower_solve(factor, innovation_block.T).T
        solved = solved - outer_rows(whitened.astype(jnp.bfloat16), rows_half)
        spot_old = lax.dynamic_slice_in_dim(solved, row_start, panel_width, 1)
        spot_new = jnp.where(row_here == row_root, whitened, spot_old)
        solved = lax.dynamic_update_slice_in_dim(solved, spot_new, row_start, 1)
        row_old = lax.dynamic_slice_in_dim(matrix, row_start, panel_width, 0)
        row_new = jnp.where((row_here == row_root) & live_columns[None, :], 0.0, row_old)
        matrix = lax.dynamic_update_slice_in_dim(matrix, row_new, row_start, 0)
        column_old = lax.dynamic_slice_in_dim(matrix, column_start, panel_width, 1)
        column_new = jnp.where(live_rows[:, None], panel_rows, column_old)
        diagonal_spot = lax.dynamic_update_slice_in_dim(column_new, factor, row_start, 0)
        column_new = jnp.where(row_here == row_root, diagonal_spot, column_new)
        column_new = jnp.where(column_here == column_root, column_new, column_old)
        matrix = lax.dynamic_update_slice_in_dim(matrix, column_new, column_start, 1)
    return (matrix, solved)


def solution(mesh):
    placed = (P("row", "col"), P("row", None, "col"), P(), P())
    return jax.shard_map(
        per_device,
        mesh=mesh,
        in_specs=placed,
        out_specs=(P("row", "col"), P("col", "row")),
        check_vma=False,
    )
```

profile of v0, /device:TPU:0, one launch (start us, length us, event | category | flops | bytes accessed | tf_op | source)
XLA Modules:
  0.0 469.5 jit_solution(13405228891102686264)
XLA Ops:
  7.2 2.0 copy.81
  9.2 5.2 %all-to-all-start = ((f32[64,8,256]{2,0,1:T(8,128)}), f32[64,8,256]{2,0,1:T(8,128)S(1)}, u32[]{:S(2)}, u32[]{:S(2)}) async-start(f32[64,8,256]{2,0,1:T(8,128)} %copy.81), calls=%async_computation | async-start | bytes 1048576 | tf_op jit(solution)/shard_map/all_to_all | solution.py:37
  18.3 9.3 %copy.69 = f32[1024,2048]{0,1:T(8,128)} copy(f32[1024,2048]{1,0:T(8,128)} %param.11) | data formatting | bytes 16777216 | tf_op args[0]
  27.6 2.3 dynamic-slice_select_fusion.3
  30.0 1.3 copy.82
  31.3 4.9 %all-to-all-start.1 = ((f32[512,1,256]{2,1,0:T(1,128)}), f32[512,1,256]{2,1,0:T(1,128)S(1)}, u32[]{:S(2)}, u32[]{:S(2)}) async-start(f32[512,1,256]{2,1,0:T(1,128)} %copy.82), calls=%async_computation.1 | async-start | bytes 1048576 | tf_op jit(solution)/shard_map/all_to_all | solution.py:36
  36.2 3.2 dynamic-slice_select_fusion.1
  39.4 55.2 %all-reduce.8.cloned.1.call-done = f32[1024,256]{0,1:T(8,128)} async-done(((f32[1024,256]{0,1:T(8,128)}), f32[1024,256]{0,1:T(8,128)}) %all-reduce.8.cloned.1.call-update) | async-done | bytes 1048592 | tf_op jit(solution)/shard_map/psum | solution.py:13
  94.5 1.7 dynamic-slice_select_fusion.7
  100.2 61.6 %all-reduce.14.cloned.1.call-done = (f32[256,2048]{0,1:T(8,128)}, f32[256,256]{0,1:T(8,128)}, f32[256,128]{1,0:T(8,128)}) async-done(((f32[256,2048]{0,1:T(8,128)}, f32[256,256]{0,1:T(8,128)}, f32[256,128]{1,0:T(8,128)}), (f32[256,2048]{0,1:T(8,128)}, f32[256,256]{0,1:T(8,128)}, f32[256,128]{1,0:T(8,128)})) %all-reduce.14.cloned.1.call-update) | async-done | bytes 2490384 | tf_op jit(solution)/shard_map/psum | solution.py:13
  161.8 1.1 copy.59
  163.9 11.7 %cholesky.130 = f32[128,128]{1,0:T(8,128)S(1)} custom-call(f32[128,128]{1,0:T(8,128)S(1)} %cholesky.194), custom_call_target="Cholesky" | custom-call | tf_op jit(solution)/shard_map/jit(cholesky)/cholesky | solution.py:71
  175.6 9.8 %custom-call.21 = f32[1,128,128]{1,2,0:T(8,128)S(1)} custom-call(f32[1,128,128]{2,1,0:T(8,128)S(1)} %get-tuple-element.163), custom_call_target="InvertDiagBlocksLowerTriangular" | custom-call | tf_op jit(solution)/shard_map/jit(cholesky)/cholesky | solution.py:71
  185.9 11.7 %cholesky.147 = f32[128,128]{1,0:T(8,128)S(1)} custom-call(f32[128,128]{1,0:T(8,128)S(1)} %convolution_subtract_fusion.11), custom_call_target="Cholesky" | custom-call | tf_op jit(solution)/shard_map/jit(cholesky)/cholesky | solution.py:71
  200.1 4.6 while.12
  201.2 1.3 dynamic-slice.26
  203.2 1.3 dynamic-slice.26
  204.7 19.7 %custom-call.22 = f32[2,128,128]{1,2,0:T(8,128)S(1)} custom-call(f32[2,128,128]{2,1,0:T(8,128)S(1)} %get-tuple-element.48), custom_call_target="InvertDiagBlocksLowerTriangular" | custom-call | tf_op jit(solution)/shard_map/jit(_solve_triangular)/triangular_solve | solution.py:17
  224.4 2.3 fusion.6
  226.7 3.1 convolution_subtract_fusion.3
  229.7 1.0 copy.67
  231.0 1.7 fusion.18
  232.7 1.7 convolution_subtract_fusion.7
  236.1 4.3 convolution_subtract_fusion.1
  241.4 3.4 copy-done
  244.8 1.1 dynamic-slice_select_fusion.2
  247.8 3.0 dynamic-slice_select_fusion
  250.8 46.6 %all-reduce.10.cloned.1.call-done = f32[1024,256]{0,1:T(8,128)} async-done(((f32[1024,256]{0,1:T(8,128)}), f32[1024,256]{0,1:T(8,128)}) %all-reduce.10.cloned.1.call-update) | async-done | bytes 1048592 | tf_op jit(solution)/shard_map/psum | solution.py:13
  297.4 1.7 dynamic-slice_select_fusion.6
  299.3 65.3 %all-reduce.12.cloned.1.call-done = (f32[256,2048]{0,1:T(8,128)}, f32[256,256]{0,1:T(8,128)}, f32[256,128]{1,0:T(8,128)}) async-done(((f32[256,2048]{0,1:T(8,128)}, f32[256,256]{0,1:T(8,128)}, f32[256,128]{1,0:T(8,128)}), (f32[256,2048]{0,1:T(8,128)}, f32[256,256]{0,1:T(8,128)}, f32[256,128]{1,0:T(8,128)})) %all-reduce.12.cloned.1.call-update) | async-done | bytes 2490384 | tf_op jit(solution)/shard_map/psum | solution.py:13
  364.6 1.1 copy.71
  366.7 11.7 %cholesky.164 = f32[128,128]{1,0:T(8,128)S(1)} custom-call(f32[128,128]{1,0:T(8,128)S(1)} %cholesky.197), custom_call_target="Cholesky" | custom-call | tf_op jit(solution)/shard_map/jit(cholesky)/cholesky | solution.py:71
  378.4 9.8 %custom-call.24 = f32[1,128,128]{1,2,0:T(8,128)S(1)} custom-call(f32[1,128,128]{2,1,0:T(8,128)S(1)} %get-tuple-element.161), custom_call_target="InvertDiagBlocksLowerTriangular" | custom-call | tf_op jit(solution)/shard_map/jit(cholesky)/cholesky | solution.py:71
  388.7 11.7 %cholesky.181 = f32[128,128]{1,0:T(8,128)S(1)} custom-call(f32[128,128]{1,0:T(8,128)S(1)} %convolution_subtract_fusion.10), custom_call_target="Cholesky" | custom-call | tf_op jit(solution)/shard_map/jit(cholesky)/cholesky | solution.py:71
  403.5 4.4 while.13
  404.3 1.4 dynamic-slice.28
  406.4 1.4 dynamic-slice.28
  407.9 19.7 %custom-call.25 = f32[2,128,128]{1,2,0:T(8,128)S(1)} custom-call(f32[2,128,128]{2,1,0:T(8,128)S(1)} %get-tuple-element.50), custom_call_target="InvertDiagBlocksLowerTriangular" | custom-call | tf_op jit(solution)/shard_map/jit(_solve_triangular)/triangular_solve | solution.py:17
  427.6 2.3 fusion.4
  429.9 3.1 convolution_subtract_fusion.2
  433.0 1.0 copy.78
  434.8 1.7 fusion.16
  438.2 1.0 copy.89
  440.2 6.2 %convolution_subtract_fusion = f32[1024,2048]{0,1:T(8,128)} fusion(f32[1024,2048]{0,1:T(8,128)} %copy-done, bf16[128,2048]{0,1:T(8,128)(2,1)S(1)} %fusion.43, bf16[128,2048]{0,1:T(8,128)(2,1)S(1)} %copy-done.1, pred[2048]{0:T(1024)(128)(4,1)S(1)} %gt.75, f32[128,1024]{1,0:T(8,128)S(1)} %fusion.44, f32[128,1024]{1,0:T(8,128)S(1)} %fusion.16, ...), kind=kOutput, calls=%fused_computation.4 | convolution fusion | flops 1079771136 | bytes 18877440 | tf_op jit(solution)/shard_map/dot_general | solution.py:21
  446.4 3.3 select_dynamic-update-slice_fusion
  449.7 1.4 dynamic-slice_select_fusion.4
  451.2 2.4 select_dynamic-update-slice_fusion.2
  453.6 9.1 %copy.88 = f32[1024,2048]{1,0:T(8,128)} copy(f32[1024,2048]{0,1:T(8,128)} %select_dynamic-update-slice_fusion.2) | data formatting | bytes 16777216
  (109 shorter events, 19.4 us)
Async XLA Ops:
  7.2 7.9 %copy-start.6 = (s32[32]{0:T(128)S(1)}, s32[32]{0:T(128)}, u32[]{:S(2)}) copy-start(s32[32]{0:T(128)} %param.13) | copy-start | bytes 388
  9.2 20.8 %all-to-all-start = ((f32[64,8,256]{2,0,1:T(8,128)}), f32[64,8,256]{2,0,1:T(8,128)S(1)}, u32[]{:S(2)}, u32[]{:S(2)}) async-start(f32[64,8,256]{2,0,1:T(8,128)} %copy.81), calls=%async_computation | async-start | bytes 1048576 | tf_op jit(solution)/shard_map/all_to_all | solution.py:37
  14.4 80.1 %all-reduce.8.cloned.1.call-start = ((), (), s32[]{:S(2)}) async-start(), calls=%async_computation.2 | async-start | bytes 2097152 | tf_op jit(solution)/shard_map/psum | solution.py:13
  31.3 64.9 %all-to-all-start.1 = ((f32[512,1,256]{2,1,0:T(1,128)}), f32[512,1,256]{2,1,0:T(1,128)S(1)}, u32[]{:S(2)}, u32[]{:S(2)}) async-start(f32[512,1,256]{2,1,0:T(1,128)} %copy.82), calls=%async_computation.1 | async-start | bytes 1048576 | tf_op jit(solution)/shard_map/all_to_all | solution.py:36
  36.2 125.6 %all-reduce.14.cloned.1.call-start = ((), (), s32[]{:S(2)}) async-start(), calls=%async_computation.5 | async-start | bytes 4980736 | tf_op jit(solution)/shard_map/psum | solution.py:13
  97.1 200.3 %all-reduce.10.cloned.1.call-start = ((), (), s32[]{:S(2)}) async-start(), calls=%async_computation.3 | async-start | bytes 2097152 | tf_op jit(solution)/shard_map/psum | solution.py:13
  226.6 4.1 copy-start.4
  232.7 3.4 copy-start.2
  241.4 3.4 copy-start
  245.9 118.6 %all-reduce.12.cloned.1.call-start = ((), (), s32[]{:S(2)}) async-start(), calls=%async_computation.4 | async-start | bytes 4980736 | tf_op jit(solution)/shard_map/psum | solution.py:13
  429.9 4.1 copy-start.5
  434.0 2.6 copy-start.3
  438.2 2.0 copy-start.1
Sparse Core Ops, SparseCore 0:
  30.1 64.3 all-reduce.7
  98.6 63.1 all-reduce.13
  246.1 51.2 all-reduce.9
  301.4 63.1 all-reduce.11
where the time goes:
time: 473 us; the launch traced here: 469 us
  waiting for transfers between devices  229 us (48%)
  other arithmetic  133 us (28%)
  local copies, waits for them, and re-layouts  39.7 us (8%)
  matrix products  33.4 us (7%)
  between operations  22.7 us (5%)
  starting transfers between devices  10.7 us (2%)
    psum x4, waiting for transfers between devices, spread(): return lax.psum(kept, axis)  229 us
    another operation x13, other arithmetic, per_device(): factor = jnp.linalg.cholesky(diagonal)  68.6 us
    another operation x5, other arithmetic, lower_solve(): return jax.scipy.linalg.solve_triangular(factor, right_side, lower=True)  39.4 us
    unnamed x19, local copies, waits for them, and re-layouts  24.8 us
    another operation x18, matrix products, lower_solve(): return jax.scipy.linalg.solve_triangular(factor, right_side, lower=True)  21.3 us
    select_n x6, other arithmetic, spread(): jnp.where(lax.axis_index(axis) == source, value, 0).astype(value.dtype)  13 us
    dot_general x4, matrix products, outer_rows(): lax.dot_general(left, right, CONTRACT_LAST, preferred_element_type=jnp.fl...  11.2 us
    another operation x25, local copies, waits for them, and re-layouts, lower_solve(): return jax.scipy.linalg.solve_triangular(factor, right_side, lower=True)  10.2 us
  transfers between devices with their start and end apart: 6, of which 4 were waited for; matrix products, arithmetic and copies ran while one was open for 5% of the time, Pallas kernels for 0%

commit v1 on v0

--- a/solution.py
+++ b/solution.py
@@ -10,7 +10,7 @@
 
 def spread(value, axis, source):
     kept = jnp.where(lax.axis_index(axis) == source, value, 0).astype(value.dtype)
-    return lax.psum(kept, axis)
+    return jnp.sum(lax.all_gather(kept, axis), axis=0)
 
 
 def lower_solve(factor, right_side):

time: 473 us -> 509 us (1.076)
  waiting for transfers between devices: 229 us -> 266 us
  other arithmetic: 133 us -> 150 us
  local copies, waits for them, and re-layouts: 39.7 us -> 23.6 us
  blocking collectives: 0 us -> 13.6 us
  matrix products: 33.4 us -> 23.3 us
  starting transfers between devices: 10.7 us -> 5.33 us
    all_gather x0 -> x8, waiting for transfers between devices: none -> 256 us  [spread(): return jnp.sum(lax.all_gather(kept, axis), axis=0)]
    psum x4 -> x0, waiting for transfers between devices: 229 us -> none  [spread(): return lax.psum(kept, axis)]
    reduce_sum x0 -> x8, other arithmetic: none -> 24.7 us  [spread(): return jnp.sum(lax.all_gather(kept, axis), axis=0)]
    all_to_all x0 -> x1, blocking collectives: none -> 13.6 us  [per_device(): lax.all_to_all(innovations, 'row', split_axis=1, concat_axis=0, tiled=True)]
    unnamed x19 -> x31, local copies, waits for them, and re-layouts: 24.8 us -> 13.4 us
    all_to_all x1, waiting for transfers between devices: 0.01 us -> 9.94 us  [per_device(): lax.all_to_all(lax.all_to_all(innovations, 'row', split_axis=1, concat_ax...]
    another operation x18, matrix products: 21.3 us -> 12.3 us  [lower_solve(): return jax.scipy.linalg.solve_triangular(factor, right_side, lower=True)]
    all_to_all x1 -> x0, starting transfers between devices: 5.2 us -> none  [per_device(): lax.all_to_all(innovations, 'row', split_axis=1, concat_axis=0, tiled=True)]
  transfers between devices with their start and end apart: 6 -> 9, of which waited for: 4 -> 8; matrix products, arithmetic and copies ran while one was open for 5% -> 32% of each run, Pallas kernels for 0% -> 0%
where the time goes in v1:
time: 509 us; the launch traced here: 506 us
  waiting for transfers between devices  266 us (52%)
  other arithmetic  150 us (29%)
  local copies, waits for them, and re-layouts  23.6 us (5%)
  matrix products  23.3 us (5%)
  between operations  23.2 us (5%)
  blocking collectives  13.6 us (3%)
  starting transfers between devices  5.33 us (1%)
    all_gather x8, waiting for transfers between devices, spread(): return jnp.sum(lax.all_gather(kept, axis), axis=0)  256 us
    another operation x13, other arithmetic, per_device(): factor = jnp.linalg.cholesky(diagonal)  68.5 us
    another operation x5, other arithmetic, lower_solve(): return jax.scipy.linalg.solve_triangular(factor, right_side, lower=True)  39.4 us
    reduce_sum x8, other arithmetic, spread(): return jnp.sum(lax.all_gather(kept, axis), axis=0)  24.7 us
    all_to_all x1, blocking collectives, per_device(): lax.all_to_all(innovations, 'row', split_axis=1, concat_axis=0, tiled=True)  13.6 us
    unnamed x31, local copies, waits for them, and re-layouts  13.4 us
    select_n x8, other arithmetic, spread(): jnp.where(lax.axis_index(axis) == source, value, 0).astype(value.dtype)  12.5 us
    another operation x18, matrix products, lower_solve(): return jax.scipy.linalg.solve_triangular(factor, right_side, lower=True)  12.3 us
  transfers between devices with their start and end apart: 9, of which 8 were waited for; matrix products, arithmetic and copies ran while one was open for 32% of the time, Pallas kernels for 0%

profile of v1, /device:TPU:0, one launch (start us, length us, event | category | flops | bytes accessed | tf_op | source)
XLA Modules:
  0.0 505.9 jit_solution(16445608573165710677)
XLA Ops:
  7.9 1.3 fusion.52
  11.8 2.3 dynamic-slice_select_fusion.3
  14.2 83.5 %all-gather.17.cloned.1.call-done = f32[4096,256]{1,0:T(8,128)} async-done(((f32[1024,256]{1,0:T(8,128)}), f32[4096,256]{1,0:T(8,128)}) %all-gather.17.cloned.1.call-update) | async-done | bytes 4194320 | tf_op jit(solution)/shard_map/all_gather | solution.py:13
  97.7 2.6 reduce_sum.91
  101.1 3.1 dynamic-slice_select_fusion.1
  105.5 13.6 %all_to_all.33 = f32[64,8,256]{2,0,1:T(8,128)S(1)} all-to-all(f32[64,8,256]{2,0,1:T(8,128)S(1)} %copy.34), channel_id=1, replica_groups=mesh['row'=8,'col'=4] {'row'}, dimensions={1} | all-to-all | bytes 1048576 | tf_op jit(solution)/shard_map/all_to_all | solution.py:37
  119.1 1.3 copy.35
  120.4 4.4 all-to-all-start.1
  128.3 9.9 %all-to-all-done.1 = f32[512,1,256]{2,1,0:T(1,128)S(1)} async-done(((f32[512,1,256]{2,1,0:T(1,128)}), f32[512,1,256]{2,1,0:T(1,128)S(1)}, u32[]{:S(2)}, u32[]{:S(2)}) %all-to-all-start.1) | async-done | bytes 524320 | tf_op jit(solution)/shard_map/all_to_all | solution.py:36
  139.4 1.8 reduce_sum.92
  141.4 11.7 %cholesky.130 = f32[128,128]{1,0:T(8,128)S(1)} custom-call(f32[128,128]{1,0:T(8,128)S(1)} %cholesky.194), custom_call_target="Cholesky" | custom-call | tf_op jit(solution)/shard_map/jit(cholesky)/cholesky | solution.py:71
  153.2 9.8 %custom-call.21 = f32[1,128,128]{1,2,0:T(8,128)S(1)} custom-call(f32[1,128,128]{2,1,0:T(8,128)S(1)} %get-tuple-element.89), custom_call_target="InvertDiagBlocksLowerTriangular" | custom-call | tf_op jit(solution)/shard_map/jit(cholesky)/cholesky | solution.py:71
  163.5 11.7 %cholesky.147 = f32[128,128]{1,0:T(8,128)S(1)} custom-call(f32[128,128]{1,0:T(8,128)S(1)} %convolution_subtract_fusion.11), custom_call_target="Cholesky" | custom-call | tf_op jit(solution)/shard_map/jit(cholesky)/cholesky | solution.py:71
  177.2 4.0 while.12
  178.0 1.3 bitcast_dynamic-update-slice_fusion.4
  179.9 1.3 bitcast_dynamic-update-slice_fusion.4
  181.7 19.7 %custom-call.22 = f32[2,128,128]{1,2,0:T(8,128)S(1)} custom-call(f32[2,128,128]{2,1,0:T(8,128)S(1)} %get-tuple-element.48), custom_call_target="InvertDiagBlocksLowerTriangular" | custom-call | tf_op jit(solution)/shard_map/jit(_solve_triangular)/triangular_solve | solution.py:17
  203.8 21.3 %all-gather.21.cloned.1.call-done = f32[2048,2048]{1,0:T(8,128)} async-done(((f32[256,2048]{1,0:T(8,128)}), f32[2048,2048]{1,0:T(8,128)}) %all-gather.21.cloned.1.call-update) | async-done | bytes 16777232 | tf_op jit(solution)/shard_map/all_gather | solution.py:13
  225.1 7.8 %reduce_sum.93 = f32[256,2048]{1,0:T(8,128)S(1)} reduce(f32[8,256,2048]{2,1,0:T(8,128)} %bitcast.162, f32[]{:T(128)} %constant.160.clone.1), dimensions={0}, to_apply=%region_7.10 | reduce | flops 3670016 | bytes 18874372 | tf_op jit(solution)/shard_map/reduce_sum | solution.py:13
  232.9 1.1 fusion.6
  233.9 1.1 convolution_subtract_fusion.3
  235.0 1.1 fusion.40
  236.1 4.7 convolution_subtract_fusion.1
  242.3 3.4 copy-done
  245.7 1.1 dynamic-slice_select_fusion.2
  247.4 3.0 all-gather.29.cloned.1.call-done
  250.4 1.4 copy.47
  254.0 78.6 %all-gather.23.cloned.1.call-done = f32[4096,256]{1,0:T(8,128)} async-done(((f32[1024,256]{1,0:T(8,128)}), f32[4096,256]{1,0:T(8,128)}) %all-gather.23.cloned.1.call-update) | async-done | bytes 4194320 | tf_op jit(solution)/shard_map/all_gather | solution.py:13
  332.5 2.6 reduce_sum.95
  335.9 3.2 dynamic-slice_select_fusion
  339.9 16.4 %all-gather.31.cloned.1.call-done = f32[1024,256]{0,1:T(8,128)} async-done(((f32[128,256]{0,1:T(8,128)}), f32[1024,256]{0,1:T(8,128)}) %all-gather.31.cloned.1.call-update) | async-done | bytes 1048592 | tf_op jit(solution)/shard_map/all_gather | solution.py:13
  356.3 1.4 copy.48
  358.0 28.6 %all-gather.25.cloned.1.call-done = f32[2048,256]{1,0:T(8,128)} async-done(((f32[256,256]{1,0:T(8,128)}), f32[2048,256]{1,0:T(8,128)}) %all-gather.25.cloned.1.call-update) | async-done | bytes 2097168 | tf_op jit(solution)/shard_map/all_gather | solution.py:13
  386.5 1.8 reduce_sum.96
  388.5 11.7 %cholesky.164 = f32[128,128]{1,0:T(8,128)S(1)} custom-call(f32[128,128]{1,0:T(8,128)S(1)} %cholesky.197), custom_call_target="Cholesky" | custom-call | tf_op jit(solution)/shard_map/jit(cholesky)/cholesky | solution.py:71
  400.3 9.8 %custom-call.24 = f32[1,128,128]{1,2,0:T(8,128)S(1)} custom-call(f32[1,128,128]{2,1,0:T(8,128)S(1)} %get-tuple-element.85), custom_call_target="InvertDiagBlocksLowerTriangular" | custom-call | tf_op jit(solution)/shard_map/jit(cholesky)/cholesky | solution.py:71
  410.6 11.7 %cholesky.181 = f32[128,128]{1,0:T(8,128)S(1)} custom-call(f32[128,128]{1,0:T(8,128)S(1)} %convolution_subtract_fusion.10), custom_call_target="Cholesky" | custom-call | tf_op jit(solution)/shard_map/jit(cholesky)/cholesky | solution.py:71
  425.0 4.2 while.13
  425.7 1.4 bitcast_dynamic-update-slice_fusion.5
  427.7 1.4 bitcast_dynamic-update-slice_fusion.5
  429.1 19.7 %custom-call.25 = f32[2,128,128]{1,2,0:T(8,128)S(1)} custom-call(f32[2,128,128]{2,1,0:T(8,128)S(1)} %get-tuple-element.50), custom_call_target="InvertDiagBlocksLowerTriangular" | custom-call | tf_op jit(solution)/shard_map/jit(_solve_triangular)/triangular_solve | solution.py:17
  453.4 24.8 %all-gather.27.cloned.1.call-done = f32[2048,2048]{1,0:T(8,128)} async-done(((f32[256,2048]{1,0:T(8,128)}), f32[2048,2048]{1,0:T(8,128)}) %all-gather.27.cloned.1.call-update) | async-done | bytes 16777232 | tf_op jit(solution)/shard_map/all_gather | solution.py:13
  478.3 7.8 %reduce_sum.97 = f32[256,2048]{1,0:T(8,128)S(1)} reduce(f32[8,256,2048]{2,1,0:T(8,128)} %bitcast.163, f32[]{:T(128)} %constant.160.clone.1), dimensions={0}, to_apply=%region_11.15 | reduce | flops 3670016 | bytes 18874372 | tf_op jit(solution)/shard_map/reduce_sum | solution.py:13
  486.0 1.1 fusion.4
  487.1 1.1 convolution_subtract_fusion.2
  488.1 1.1 fusion.43
  489.2 4.7 convolution_subtract_fusion
  495.5 3.4 copy-done.1
  (122 shorter events, 25.2 us)
Async XLA Ops:
  7.2 90.5 %all-gather.17.cloned.1.call-start = ((), (), s32[]{:S(2)}) async-start(), calls=%async_computation.2 | async-start | bytes 5242880 | tf_op jit(solution)/shard_map/all_gather | solution.py:13
  14.1 125.3 %all-gather.19.cloned.1.call-start = ((), (), s32[]{:S(2)}) async-start(), calls=%async_computation.3 | async-start | bytes 2359296 | tf_op jit(solution)/shard_map/all_gather | solution.py:13
  101.1 124.0 %all-gather.21.cloned.1.call-start = ((), (), s32[]{:S(2)}) async-start(), calls=%async_computation.4 | async-start | bytes 18874368 | tf_op jit(solution)/shard_map/all_gather | solution.py:13
  104.2 1.0 copy-start.8
  105.3 22.0 %copy-start.9 = (s32[32]{0:T(128)S(1)}, s32[32]{0:T(128)}, u32[]{:S(2)}) copy-start(s32[32]{0:T(128)} %param.13) | copy-start | bytes 388
  120.4 17.8 %all-to-all-start.1 = ((f32[512,1,256]{2,1,0:T(1,128)}), f32[512,1,256]{2,1,0:T(1,128)S(1)}, u32[]{:S(2)}, u32[]{:S(2)}) async-start(f32[512,1,256]{2,1,0:T(1,128)} %copy.35), calls=%async_computation.1 | async-start | bytes 1048576 | tf_op jit(solution)/shard_map/all_to_all | solution.py:36
  124.8 125.5 %all-gather.29.cloned.1.call-start = ((), (), s32[]{:S(2)}) async-start(), calls=%async_computation.8 | async-start | bytes 1179648 | tf_op jit(solution)/shard_map/all_gather | solution.py:13
  138.4 3.0 copy-start.2
  139.2 193.4 %all-gather.23.cloned.1.call-start = ((), (), s32[]{:S(2)}) async-start(), calls=%async_computation.5 | async-start | bytes 5242880 | tf_op jit(solution)/shard_map/all_gather | solution.py:13
  175.2 26.2 %copy-start.6 = (f32[256,256]{1,0:T(8,128)}, f32[256,256]{1,0:T(8,128)S(1)}, u32[]{:S(2)}) copy-start(f32[256,256]{1,0:T(8,128)S(1)} %get-tuple-element.87) | copy-start | bytes 786436
  181.2 0.6 copy-start.11
  241.0 1.0 copy-start.7
  242.3 3.4 copy-start
  246.8 6.0 %copy-start.3 = (f32[128,1,4,256]{0,3,2,1:T(8,128)S(1)}, f32[128,1,4,256]{0,3,2,1:T(8,128)}, u32[]{:S(2)}) copy-start(f32[128,1,4,256]{0,3,2,1:T(8,128)} %copy-done.2) | copy-start | bytes 1572868
  246.9 109.4 %all-gather.31.cloned.1.call-start = ((), (), s32[]{:S(2)}) async-start(), calls=%async_computation.9 | async-start | bytes 1179648 | tf_op jit(solution)/shard_map/all_gather | solution.py:13
  253.9 132.6 %all-gather.25.cloned.1.call-start = ((), (), s32[]{:S(2)}) async-start(), calls=%async_computation.6 | async-start | bytes 2359296 | tf_op jit(solution)/shard_map/all_gather | solution.py:13
  335.9 142.4 %all-gather.27.cloned.1.call-start = ((), (), s32[]{:S(2)}) async-start(), calls=%async_computation.7 | async-start | bytes 18874368 | tf_op jit(solution)/shard_map/all_gather | solution.py:13
  339.1 0.7 copy-start.10
  388.3 36.6 %copy-start.12 = (s32[2,2]{1,0:T(2,128)S(1)}, s32[2,2]{1,0:T(2,128)}, u32[]{:S(2)}) copy-start(s32[2,2]{1,0:T(2,128)} %copy-done.11) | copy-start | bytes 52
  423.0 25.8 %copy-start.4 = (f32[256,256]{1,0:T(8,128)}, f32[256,256]{1,0:T(8,128)S(1)}, u32[]{:S(2)}) copy-start(f32[256,256]{1,0:T(8,128)S(1)} %get-tuple-element.83) | copy-start | bytes 786436
  494.2 1.0 copy-start.5
  495.5 3.4 copy-start.1
Sparse Core Ops, SparseCore 0:
  14.2 83.4 all-gather.16
  101.2 31.5 all-gather.18
  135.2 89.8 all-gather.20
  226.8 23.4 all-gather.28
  251.8 80.7 all-gather.22
  334.3 21.9 all-gather.30
  358.7 27.7 all-gather.24
  388.4 89.7 all-gather.26
